TPU v7x, 128 devices: a whole 4x4x4 slice. The times are simulated.
128 devices in a mesh: dp: 4 (over z), latent: 32 (over x, y, core).
Axes of the slice: x: 4, y: 4, z: 4, core: 2. Of those that a mesh axis runs over, the one named last changes fastest.
Arguments:
- acts: bfloat16 [640, 8192], P(('dp', 'latent')), may hold values from -6 to 6
- chat_len: int32 [128], P(('dp', 'latent')), may hold values from 1 to 5, as said below
- group_of: int32 [640, 1], P(('dp', 'latent')), may hold values from 0 to 4; in each aligned block of 5 rows (0 to 4, 5 to 9, ...) no two rows name the same one
- w_enc: bfloat16 [2, 4096, 16384], P(None, None, 'latent'), may hold values from -0.0625 to 0.0625
- b_enc: float32 [16384], P('latent'), may hold values from -3 to 3
- w_dec: bfloat16 [16384, 8192], P('latent'), may hold values from -0.046875 to 0.046875
- b_dec: float32 [2, 4096], replicated, may hold values from -3 to 3
Outputs:
- grad_enc: bfloat16 [2, 4096, 16384], P(None, 'dp', 'latent')
- grad_dec: bfloat16 [16384, 8192], P('latent', 'dp')
- loss: float32 [], replicated
Inputs may be any that keep to these rules, and one draw needn't show every extreme that they name: `chat_len`: the last serving shard harvests all 5 rows. `group_of`: among the 5 row slots of each serving shard every value 0 to 4 appears exactly once.
All inputs are finite; a program needn't handle non-finite values.
Results may differ from a plain program's by a relative error of at most 0.02.
Values may be sent and summed in bfloat16 or wider, within the bound.
No kernel may reach another device: no remote copies, remote signals or barrier semaphores. Data moves between devices by JAX's collectives and lax.ppermute only.
A program may use at most 128 MiB of HBM per device.

v0:
```python
import jax
import jax.numpy as jnp
from jax import lax
from jax.sharding import PartitionSpec as P

sparsity_weight = 1.0
loss_scale = 8.0
norm_eps = 1e-06


def shards(acts, chat_len, group_of, w_enc, b_enc, w_dec, b_dec):
    groups = lax.axis_size("dp")
    slots = acts.shape[0]
    width = acts.shape[1]
    half = width // 2
    local_latents = w_enc.shape[2]
    capacity = slots // (groups + 1)
    slot_ids = jnp.arange(slots, dtype=jnp.int32)
    alive = (slot_ids < chat_len[0]).astype(jnp.float32)
    order = jnp.argsort(group_of[:, 0], stable=True)[: groups * capacity]
    own_count = jnp.sum(alive[order])
    outgoing = acts[order].reshape(groups, capacity, width)
    out_mask = alive[order].reshape(groups, capacity).astype(jnp.bfloat16)
    received, recv_mask = (
        lax.all_to_all(outgoing, "dp", split_axis=0, concat_axis=0, tiled=True),
        lax.all_to_all(out_mask, "dp", split_axis=0, concat_axis=0, tiled=True),
    )
    member_rows, member_mask = (
        lax.all_gather(received, "latent", axis=0, tiled=True),
        lax.all_gather(recv_mask, "latent", axis=0, tiled=True),
    )
    xg = member_rows.reshape(-1, width)
    maskg = member_mask.reshape(-1).astype(jnp.float32)
    total_rows = xg.shape[0]
    share_rows = total_rows // lax.axis_size("latent")
    first_row = lax.axis_index("latent") * share_rows
    wenc_flat = w_enc.reshape(width, local_latents)
    squares_dec = jnp.square(w_dec.astype(jnp.float32))
    norm_base = jnp.sqrt(jnp.sum(squares_dec[:, :half], axis=1) + norm_eps)
    norm_inst = jnp.sqrt(jnp.sum(squares_dec[:, half:], axis=1) + norm_eps)
    norm_sum = norm_base + norm_inst
    column_ids = jnp.arange(width, dtype=jnp.int32)
    bias_row = b_dec.reshape(width)
    pre = jnp.dot(xg, wenc_flat, preferred_element_type=jnp.float32) + b_enc[None, :]
    act = jnp.maximum(pre, 0.0)
    feats = act * act
    feats16 = feats.astype(jnp.bfloat16)
    partial_value = jnp.dot(feats16, w_dec, preferred_element_type=jnp.float32)
    recon = lax.psum(partial_value.astype(jnp.bfloat16), "latent").astype(jnp.float32)
    err = (recon + bias_row[None, :] - xg.astype(jnp.float32)) * maskg[:, None]
    err16 = err.astype(jnp.bfloat16)
    err_share = lax.dynamic_slice_in_dim(err, first_row, share_rows, 0)
    square_sum = jnp.sum(err_share * err_share)
    feat_sum = jnp.sum(feats * maskg[:, None], axis=0)
    local_loss = square_sum + sparsity_weight * jnp.sum(feat_sum * norm_sum)
    dfeat = 2.0 * lax.dot_general(
        err16, w_dec, (((1,), (1,)), ((), ())), preferred_element_type=jnp.float32
    )
    dfeat = dfeat + sparsity_weight * maskg[:, None] * norm_sum[None, :]
    dpre16 = (dfeat * 2.0 * act).astype(jnp.bfloat16)
    enc_term = lax.dot_general(
        xg, dpre16, (((0,), (0,)), ((), ())), preferred_element_type=jnp.float32
    )
    enc_term = enc_term.reshape(2, half, local_latents)
    dec_term = 2.0 * lax.dot_general(
        feats16, err16, (((0,), (0,)), ((), ())), preferred_element_type=jnp.float32
    )
    scale = jnp.where(
        column_ids[None, :] < half, (feat_sum / norm_base)[:, None], (feat_sum / norm_inst)[:, None]
    )
    dec_term = dec_term + sparsity_weight * scale * w_dec.astype(jnp.float32)
    enc_total = lax.psum_scatter(
        enc_term.astype(jnp.bfloat16), "dp", scatter_dimension=1, tiled=True
    ).astype(jnp.float32)
    dec_total = lax.psum_scatter(
        dec_term.astype(jnp.bfloat16), "dp", scatter_dimension=1, tiled=True
    ).astype(jnp.float32)
    total, count = lax.psum((local_loss, own_count), ("dp", "latent"))
    factor = loss_scale / count
    grad_enc = (enc_total * factor).astype(jnp.bfloat16)
    grad_dec = (dec_total * factor).astype(jnp.bfloat16)
    loss = total / (count * width)
    return (grad_enc, grad_dec, loss)


def solution(mesh):
    return jax.shard_map(
        shards,
        mesh=mesh,
        in_specs=(
            P(("dp", "latent"), None),
            P(("dp", "latent")),
            P(("dp", "latent"), None),
            P(None, None, "latent"),
            P("latent"),
            P("latent", None),
            P(),
        ),
        out_specs=(P(None, "dp", "latent"), P("latent", "dp"), P()),
        check_vma=False,
    )
```

profile of v0, /device:TPU:1, one launch (start us, length us, event | category | flops | bytes accessed | tf_op | source)
XLA Modules:
  0.0 414.3 jit_solution(3964806186658669848)
XLA Ops:
  7.2 0.0 copy-start
  7.2 0.0 all-gather.3.cloned.1.call-start
  7.2 1.6 sort.17
  8.9 0.0 copy-done
  8.9 0.6 gather_fusion
  9.5 0.5 broadcast.57
  10.0 0.7 reduce.2
  10.7 0.1 reshape.95
  10.8 10.1 %all_to_all.14 = bf16[4,2,4096]{2,1,0:T(2,128)(2,1)S(1)} all-to-all(bf16[4,2,4096]{2,1,0:T(2,128)(2,1)S(1)} %reshape.95), channel_id=1, replica_groups=mesh['dp'=4,'latent'=32] {'dp'}, dimensions={0} | all-to-all | bytes 131072 | tf_op jit(solution)/shard_map/all_to_all | solution.py:25
  20.9 0.7 reshape.96
  21.6 0.0 all-gather.3.cloned.1.call-update
  22.3 0.6 gather_fusion.1
  23.0 0.6 fusion.25
  23.6 0.7 copy.17
  24.3 3.2 all-to-all-start.1
  27.5 0.0 all-reduce.4.cloned.1.call-start
  27.5 1.3 dynamic-slice
  29.6 1.9 all-to-all-done.1
  31.5 0.1 reduce.1
  31.6 0.2 dynamic-update-slice
  31.8 65.9 %all-reduce = bf16[128]{0:T(256)(128)(2,1)S(1)} all-reduce(bf16[128]{0:T(256)(128)(2,1)S(1)} %dynamic-update-slice), channel_id=2, replica_groups=mesh['dp'=4,'latent'=32] {'latent'}, use_global_device_ids=true, to_apply=%add | all-reduce | flops 128 | bytes 512
  97.7 0.0 all-gather.3.cloned.1.call-done
  97.8 7.3 %multiply_reduce_fusion = (f32[512]{0:T(512)S(1)}, f32[128,512]{1,0:T(8,128)S(1)}) fusion(f32[128]{0:T(128)S(1)} %mul.102, f32[512]{0:T(512)} %param.11, bf16[8192,512]{1,0:T(8,128)(2,1)} %bitcast.33, bf16[128,1,8192]{2,1,0:T(2,128)(2,1)} %all-gather.3.cloned.1.call-done), kind=kOutput, calls=%fused_computation.26 | convolution fusion | flops 1074068992 | bytes 10752512 | tf_op jit(solution)/shard_map/dot_general | solution.py:44
  105.1 6.0 %convolution_convert_fusion = bf16[128,8192]{1,0:T(8,128)(2,1)} fusion(bf16[512,8192]{1,0:T(8,128)(2,1)} %param.12, f32[128,512]{1,0:T(8,128)S(1)} %get-tuple-element.16), kind=kOutput, calls=%fused_computation.6 | convolution fusion | flops 1074921472 | bytes 10747904 | tf_op jit(solution)/shard_map/dot_general | solution.py:48
  111.0 0.0 all-reduce.4.cloned.1.call-update
  111.1 0.0 copy-start.2
  111.1 0.2 reduce-scatter.3.cloned.1.call-start
  111.3 11.3 %convert_multiply_fusion.1 = f32[512,8192]{1,0:T(8,128)} fusion(bf16[512,8192]{1,0:T(8,128)(2,1)} %param.12), kind=kLoop, calls=%fused_computation.3 | loop fusion | flops 8388608 | bytes 25165824 | tf_op jit(solution)/shard_map/square | solution.py:38
  122.6 0.0 copy-done.2
  122.6 6.5 %slice_reduce_fusion.1 = (f32[512]{0:T(512)S(1)}, f32[512]{0:T(512)S(1)}) fusion(f32[512,8192]{1,0:T(8,128)} %convert_multiply_fusion.1), kind=kLoop, calls=%fused_computation.8 | loop fusion | flops 4193280 | bytes 16781312 | tf_op jit(solution)/shard_map/reduce_sum | solution.py:39
  129.2 8.8 %copy.19 = bf16[128,1,8192]{0,2,1:T(8,128)(2,1)S(1)} copy(bf16[128,1,8192]{2,1,0:T(2,128)(2,1)} %all-gather.3.cloned.1.call-done) | data formatting | bytes 4194304 | tf_op jit(solution)/shard_map/dot_general | solution.py:61
  138.0 0.6 multiply_reduce_fusion.2
  138.6 75.9 %all-reduce.4.cloned.1.call-done = bf16[128,8192]{1,0:T(8,128)(2,1)} async-done(((bf16[128,8192]{1,0:T(8,128)(2,1)}), bf16[128,8192]{1,0:T(8,128)(2,1)}) %all-reduce.4.cloned.1.call-update) | async-done | bytes 2097168 | tf_op jit(solution)/shard_map/psum | solution.py:49
  214.5 8.7 %subtract_multiply_fusion = f32[128,8192]{1,0:T(8,128)} fusion(bf16[128,8192]{1,0:T(8,128)(2,1)} %all-reduce.4.cloned.1.call-done, f32[128]{0:T(128)S(1)} %mul.102, f32[8192]{0:T(1024)S(1)} %bitcast.36, bf16[128,1,8192]{2,1,0:T(2,128)(2,1)} %all-gather.3.cloned.1.call-done), kind=kLoop, calls=%fused_computation.12 | loop fusion | flops 5242880 | bytes 8421888 | tf_op jit(solution)/shard_map/mul | solution.py:50
  223.2 15.0 %convolution_convert_fusion.1 = bf16[2,4096,512]{2,1,0:T(8,128)(2,1)} fusion(bf16[2,4096,128]{2,1,0:T(8,128)(2,1)S(1)} %bitcast.34, f32[128,512]{1,0:T(8,128)S(1)} %get-tuple-element.16, bf16[512,8192]{1,0:T(8,128)(2,1)} %param.12, f32[128,8192]{1,0:T(8,128)} %subtract_multiply_fusion, f32[512]{0:T(512)S(1)} %get-tuple-element.10, f32[128]{0:T(128)S(1)} %mul.102), kind=kOutput, calls=%fused_computation.9 | convolution fusion | flops 2153119744 | bytes 23333376 | tf_op jit(solution)/shard_map/dot_general | solution.py:61
  238.2 0.0 reduce-scatter.3.cloned.1.call-update
  238.2 0.0 reduce-scatter.5.cloned.1.call-start
  238.3 9.8 %fusion.1 = bf16[512,8192]{1,0:T(8,128)(2,1)} fusion(bf16[512,8192]{1,0:T(8,128)(2,1)} %param.12, f32[512]{0:T(512)S(1)} %get-tuple-element.12, f32[512]{0:T(512)S(1)} %get-tuple-element.11, pred[8192]{0:T(1024)(128)(4,1)S(1)} %iota_compare_fusion, f32[128,8192]{1,0:T(8,128)} %subtract_multiply_fusion, f32[128,512]{1,0:T(8,128)S(1)} %get-tuple-element.16), kind=kOutput, calls=%fused_computation.5 | convolution fusion | flops 1100087296 | bytes 21245952 | tf_op jit(solution)/shard_map/dot_general | solution.py:65
  248.0 0.0 reduce-scatter.5.cloned.1.call-update
  248.1 1.6 multiply_reduce_fusion.1
  251.0 69.5 %all-reduce.1 = (f32[]{:T(128)}, f32[]{:T(128)}) all-reduce(f32[]{:T(128)} %get-tuple-element.13, f32[]{:T(128)S(6)} %add.86), channel_id=1, replica_groups=mesh['dp'=4,'latent'=32] {'dp','latent'}, use_global_device_ids=true, to_apply=%region_6.7 | all-reduce | flops 2 | bytes 16 | tf_op jit(solution)/shard_map/psum | solution.py:78
  321.8 0.0 copy-start.1
  322.5 0.0 reduce-scatter.3.cloned.1.call-done
  322.5 3.3 multiply_convert_fusion.1
  325.8 77.3 %reduce-scatter.5.cloned.1.call-done = bf16[512,2048]{1,0:T(8,128)(2,1)} async-done(((bf16[512,8192]{1,0:T(8,128)(2,1)}), bf16[512,2048]{1,0:T(8,128)(2,1)}) %reduce-scatter.5.cloned.1.call-update) | async-done | bytes 2097168 | tf_op jit(solution)/shard_map/reduce_scatter | solution.py:75
  403.2 3.4 multiply_convert_fusion
  406.6 0.0 copy-done.1
  (8 shorter events, 0.0 us)
Async XLA Ops:
  7.2 1.7 copy-start
  7.2 90.6 %all-gather.3.cloned.1.call-start = ((), (), s32[]{:S(2)}) async-start(), calls=%async_computation.4 | async-start | bytes 4325376 | tf_op jit(solution)/shard_map/all_gather | solution.py:29
  24.3 7.2 %all-to-all-start.1 = ((bf16[4,1,1]{2,1,0:T(2,128)(2,1)}), bf16[4,1,1]{2,1,0:T(2,128)(2,1)S(1)}, u32[]{:S(2)}, u32[]{:S(2)}) async-start(bf16[4,1,1]{2,1,0:T(2,128)(2,1)} %copy.17), calls=%async_computation.1 | async-start | bytes 4096 | tf_op jit(solution)/shard_map/all_to_all | solution.py:26
  27.5 187.0 %all-reduce.4.cloned.1.call-start = ((), (), s32[]{:S(2)}) async-start(), calls=%async_computation.5 | async-start | bytes 4194304 | tf_op jit(solution)/shard_map/psum | solution.py:49
  111.1 11.6 %copy-start.2 = (f32[2,4096]{1,0:T(2,128)S(1)}, f32[2,4096]{1,0:T(2,128)}, u32[]{:S(2)}) copy-start(f32[2,4096]{1,0:T(2,128)} %param.13) | copy-start | bytes 98308
  111.1 211.4 %reduce-scatter.3.cloned.1.call-start = ((), (), s32[]{:S(2)}) async-start(), calls=%async_computation.6 | async-start | bytes 10485760 | tf_op jit(solution)/shard_map/reduce_scatter | solution.py:72
  238.2 165.0 %reduce-scatter.5.cloned.1.call-start = ((), (), s32[]{:S(2)}) async-start(), calls=%async_computation.7 | async-start | bytes 10485760 | tf_op jit(solution)/shard_map/reduce_scatter | solution.py:75
  321.8 84.8 %copy-start.1 = (bf16[5,8192]{1,0:T(8,128)(2,1)S(1)}, bf16[5,8192]{1,0:T(8,128)(2,1)}, u32[]{:S(2)}) copy-start(bf16[5,8192]{1,0:T(8,128)(2,1)} %param.7) | copy-start | bytes 245764
Sparse Core Ops, SparseCore 0:
  21.8 47.3 all-gather.2
  111.2 103.2 all-reduce.3
  238.3 82.5 reduce-scatter.2
  323.2 79.8 reduce-scatter.4
where the time goes:
time: 415 us; the launch traced here: 414 us
  waiting for transfers between devices  155 us (37%)
  blocking collectives  145 us (35%)
  other arithmetic  38.6 us (9%)
  matrix products  38 us (9%)
  between operations  19.7 us (5%)
  local copies, waits for them, and re-layouts  13.6 us (3%)
    reduce_scatter x1, waiting for transfers between devices, shards(): lax.psum_scatter(dec_term.astype(jnp.bfloat16), 'dp', scatter_dimension=1...  77.3 us
    psum x1, waiting for transfers between devices, shards(): lax.psum(partial_value.astype(jnp.bfloat16), 'latent').astype(jnp.float32)  75.9 us
    psum x1, blocking collectives, shards(): total, count = lax.psum((local_loss, own_count), ('dp', 'latent'))  69.5 us
    unnamed x1, blocking collectives  65.9 us
    dot_general x1, matrix products, shards(): lax.dot_general(xg, dpre16, (((0,), (0,)), ((), ())), preferred_element_t...  15 us
    square x1, other arithmetic, shards(): squares_dec = jnp.square(w_dec.astype(jnp.float32))  11.3 us
    all_to_all x1, blocking collectives, shards(): lax.all_to_all(outgoing, 'dp', split_axis=0, concat_axis=0, tiled=True)  10.1 us
    dot_general x1, matrix products, shards(): lax.dot_general(feats16, err16, (((0,), (0,)), ((), ())), preferred_eleme...  9.77 us
  transfers between devices with their start and end apart: 5, of which 3 were waited for; matrix products, arithmetic and copies ran while one was open for 11% of the time, Pallas kernels for 0%

commit v1 on v0

--- a/solution.py
+++ b/solution.py
@@ -46,7 +46,9 @@
     feats = act * act
     feats16 = feats.astype(jnp.bfloat16)
     partial_value = jnp.dot(feats16, w_dec, preferred_element_type=jnp.float32)
-    recon = lax.psum(partial_value.astype(jnp.bfloat16), "latent").astype(jnp.float32)
+    recon = jnp.sum(lax.all_gather(partial_value.astype(jnp.bfloat16), "latent"), axis=0).astype(
+        jnp.float32
+    )
     err = (recon + bias_row[None, :] - xg.astype(jnp.float32)) * maskg[:, None]
     err16 = err.astype(jnp.bfloat16)
     err_share = lax.dynamic_slice_in_dim(err, first_row, share_rows, 0)

time: 415 us -> 521 us (1.26)
  waiting for transfers between devices: 155 us -> 242 us
  other arithmetic: 38.6 us -> 58.7 us
    all_gather x0 -> x1, waiting for transfers between devices: none -> 177 us  [shards(): lax.all_gather(partial_value.astype(jnp.bfloat16), 'latent')]
    reduce_scatter x1, waiting for transfers between devices: 77.3 us -> 0.02 us  [shards(): lax.psum_scatter(dec_term.astype(jnp.bfloat16), 'dp', scatter_dimension=1...]
    psum x1 -> x0, waiting for transfers between devices: 75.9 us -> none  [shards(): lax.psum(partial_value.astype(jnp.bfloat16), 'latent').astype(jnp.float32)]
    reduce_scatter x1, waiting for transfers between devices: 0.02 us -> 62.6 us  [shards(): lax.psum_scatter(enc_term.astype(jnp.bfloat16), 'dp', scatter_dimension=1...]
    reduce_sum x0 -> x1, other arithmetic: none -> 21.2 us  [shards(): jnp.sum(lax.all_gather(partial_value.astype(jnp.bfloat16), 'latent'), axi...]
  transfers between devices with their start and end apart: 5 -> 5, of which waited for: 3 -> 3; matrix products, arithmetic and copies ran while one was open for 11% -> 10% of each run, Pallas kernels for 0% -> 0%
where the time goes in v1:
time: 521 us
  waiting for transfers between devices  242 us (46%)
  blocking collectives  144 us (28%)
  other arithmetic  58.7 us (11%)
  matrix products  36.7 us (7%)
  between operations  19.7 us (4%)
  local copies, waits for them, and re-layouts  15.6 us (3%)
    all_gather x1, waiting for transfers between devices, shards(): lax.all_gather(partial_value.astype(jnp.bfloat16), 'latent')  177 us
    psum x1, blocking collectives, shards(): total, count = lax.psum((local_loss, own_count), ('dp', 'latent'))  68.1 us
    unnamed x1, blocking collectives  65.9 us
    reduce_scatter x1, waiting for transfers between devices, shards(): lax.psum_scatter(enc_term.astype(jnp.bfloat16), 'dp', scatter_dimension=1...  62.6 us
    reduce_sum x1, other arithmetic, shards(): jnp.sum(lax.all_gather(partial_value.astype(jnp.bfloat16), 'latent'), axi...  21.2 us
    dot_general x1, matrix products, shards(): lax.dot_general(xg, dpre16, (((0,), (0,)), ((), ())), preferred_element_t...  15 us
    square x1, other arithmetic, shards(): squares_dec = jnp.square(w_dec.astype(jnp.float32))  12.9 us
  transfers between devices with their start and end apart: 5, of which 3 were waited for; matrix products, arithmetic and copies ran while one was open for 10% of the time, Pallas kernels for 0%

profile of v1, /device:TPU:1, one launch (start us, length us, event | category | flops | bytes accessed | tf_op | source)
XLA Modules:
  0.0 520.7 jit_solution(2419714381190917674)
XLA Ops:
  7.2 0.0 copy-start
  7.2 0.0 all-gather.5.cloned.1.call-start
  7.2 1.6 sort.17
  8.9 0.0 copy-done
  8.9 0.6 gather_fusion
  9.5 0.5 broadcast.57
  10.0 0.7 reduce.3
  10.7 0.1 reshape.96
  10.8 10.1 %all_to_all.14 = bf16[4,2,4096]{2,1,0:T(2,128)(2,1)S(1)} all-to-all(bf16[4,2,4096]{2,1,0:T(2,128)(2,1)S(1)} %reshape.96), channel_id=1, replica_groups=mesh['dp'=4,'latent'=32] {'dp'}, dimensions={0} | all-to-all | bytes 131072 | tf_op jit(solution)/shard_map/all_to_all | solution.py:25
  20.9 0.7 reshape.97
  21.6 0.0 all-gather.5.cloned.1.call-update
  22.3 0.6 gather_fusion.1
  23.0 0.6 fusion.25
  23.6 0.7 copy.17
  24.3 3.2 all-to-all-start.1
  27.5 0.0 all-gather.7.cloned.1.call-start
  27.5 1.3 dynamic-slice
  29.6 1.9 all-to-all-done.1
  31.5 0.1 reduce.2
  31.6 0.2 dynamic-update-slice
  31.8 65.9 %all-reduce = bf16[128]{0:T(256)(128)(2,1)S(1)} all-reduce(bf16[128]{0:T(256)(128)(2,1)S(1)} %dynamic-update-slice), channel_id=3, replica_groups=mesh['dp'=4,'latent'=32] {'latent'}, use_global_device_ids=true, to_apply=%add | all-reduce | flops 128 | bytes 512
  97.7 0.0 all-gather.5.cloned.1.call-done
  97.8 7.3 %multiply_reduce_fusion = (f32[512]{0:T(512)S(1)}, f32[128,512]{1,0:T(8,128)S(1)}) fusion(f32[128]{0:T(128)S(1)} %mul.102, f32[512]{0:T(512)} %param.11, bf16[8192,512]{1,0:T(8,128)(2,1)} %bitcast.34, bf16[128,1,8192]{2,1,0:T(2,128)(2,1)} %all-gather.5.cloned.1.call-done), kind=kOutput, calls=%fused_computation.26 | convolution fusion | flops 1074068992 | bytes 10752512 | tf_op jit(solution)/shard_map/dot_general | solution.py:44
  105.1 0.0 copy-start.3
  105.1 6.0 %convolution_convert_fusion = bf16[128,8192]{1,0:T(8,128)(2,1)} fusion(bf16[512,8192]{1,0:T(8,128)(2,1)} %param.12, f32[128,512]{1,0:T(8,128)S(1)} %get-tuple-element.16), kind=kOutput, calls=%fused_computation.6 | convolution fusion | flops 1074921472 | bytes 10747904 | tf_op jit(solution)/shard_map/dot_general | solution.py:48
  111.0 0.0 all-gather.7.cloned.1.call-update
  111.1 0.2 reduce-scatter.5.cloned.1.call-start
  111.3 12.9 %convert_multiply_fusion.1 = f32[512,8192]{1,0:T(8,128)} fusion(bf16[512,8192]{1,0:T(8,128)(2,1)} %param.12), kind=kLoop, calls=%fused_computation.3 | loop fusion | flops 8388608 | bytes 25165824 | tf_op jit(solution)/shard_map/square | solution.py:38
  124.2 6.5 %slice_reduce_fusion.1 = (f32[512]{0:T(512)S(1)}, f32[512]{0:T(512)S(1)}) fusion(f32[512,8192]{1,0:T(8,128)} %convert_multiply_fusion.1), kind=kLoop, calls=%fused_computation.8 | loop fusion | flops 4193280 | bytes 16781312 | tf_op jit(solution)/shard_map/reduce_sum | solution.py:39
  130.7 0.6 multiply_reduce_fusion.2
  131.3 177.4 %all-gather.7.cloned.1.call-done = bf16[4096,8192]{1,0:T(8,128)(2,1)} async-done(((bf16[128,8192]{1,0:T(8,128)(2,1)}), bf16[4096,8192]{1,0:T(8,128)(2,1)}) %all-gather.7.cloned.1.call-update) | async-done | bytes 67108880 | tf_op jit(solution)/shard_map/all_gather | solution.py:49
  308.7 21.2 %reduce_sum.66 = bf16[128,8192]{1,0:T(8,128)(2,1)S(1)} reduce(bf16[32,128,8192]{2,1,0:T(8,128)(2,1)} %bitcast.5, bf16[]{:T(256)} %constant.2.clone.1), dimensions={0}, to_apply=%region_1.2 | reduce | flops 32505856 | bytes 69206016 | tf_op jit(solution)/shard_map/reduce_sum | solution.py:49
  329.9 6.1 %subtract_multiply_fusion = f32[128,8192]{1,0:T(8,128)S(1)} fusion(bf16[128,8192]{1,0:T(8,128)(2,1)S(1)} %reduce_sum.66, f32[128]{0:T(128)S(1)} %mul.102, f32[8192]{0:T(1024)S(1)} %bitcast.37, bf16[128,1,8192]{2,1,0:T(2,128)(2,1)} %all-gather.5.cloned.1.call-done), kind=kLoop, calls=%fused_computation.12 | loop fusion | flops 5242880 | bytes 8421888 | tf_op jit(solution)/shard_map/mul | solution.py:52
  336.0 0.0 copy-start.2
  336.0 1.9 copy-done.2
  338.0 8.4 %fusion.1 = bf16[512,8192]{1,0:T(8,128)(2,1)} fusion(bf16[512,8192]{1,0:T(8,128)(2,1)} %param.12, f32[512]{0:T(512)S(1)} %get-tuple-element.12, f32[512]{0:T(512)S(1)} %get-tuple-element.11, pred[8192]{0:T(1024)(128)(4,1)S(1)} %iota_compare_fusion, f32[128,8192]{1,0:T(8,128)S(1)} %subtract_multiply_fusion, f32[128,512]{1,0:T(8,128)S(1)} %get-tuple-element.16), kind=kOutput, calls=%fused_computation.5 | convolution fusion | flops 1100087296 | bytes 21245952 | tf_op jit(solution)/shard_map/dot_general | solution.py:67
  346.4 0.0 reduce-scatter.5.cloned.1.call-update
  346.4 0.3 reduce-scatter.3.cloned.1.call-start
  346.7 8.9 %copy.19 = bf16[128,1,8192]{0,2,1:T(8,128)(2,1)S(1)} copy(bf16[128,1,8192]{2,1,0:T(2,128)(2,1)} %all-gather.5.cloned.1.call-done) | data formatting | bytes 4194304 | tf_op jit(solution)/shard_map/dot_general | solution.py:63
  355.6 15.0 %convolution_convert_fusion.1 = bf16[2,4096,512]{2,1,0:T(8,128)(2,1)} fusion(bf16[2,4096,128]{2,1,0:T(8,128)(2,1)S(1)} %bitcast.35, f32[128,512]{1,0:T(8,128)S(1)} %get-tuple-element.16, bf16[512,8192]{1,0:T(8,128)(2,1)} %param.12, f32[128,8192]{1,0:T(8,128)} %copy-done.2, f32[512]{0:T(512)S(1)} %get-tuple-element.10, f32[128]{0:T(128)S(1)} %mul.102), kind=kOutput, calls=%fused_computation.9 | convolution fusion | flops 2153119744 | bytes 23333376 | tf_op jit(solution)/shard_map/dot_general | solution.py:63
  370.5 0.0 reduce-scatter.3.cloned.1.call-update
  370.5 1.6 multiply_reduce_fusion.1
  373.5 68.1 %all-reduce.1 = (f32[]{:T(128)}, f32[]{:T(128)}) all-reduce(f32[]{:T(128)} %get-tuple-element.13, f32[]{:T(128)S(6)} %add.84), channel_id=1, replica_groups=mesh['dp'=4,'latent'=32] {'dp','latent'}, use_global_device_ids=true, to_apply=%region_6.7 | all-reduce | flops 2 | bytes 16 | tf_op jit(solution)/shard_map/psum | solution.py:80
  442.9 0.0 copy-start.1
  443.6 0.0 reduce-scatter.5.cloned.1.call-done
  443.6 3.4 multiply_convert_fusion
  447.1 62.6 %reduce-scatter.3.cloned.1.call-done = bf16[2,1024,512]{2,1,0:T(8,128)(2,1)} async-done(((bf16[2,4096,512]{2,1,0:T(8,128)(2,1)}), bf16[2,1024,512]{2,1,0:T(8,128)(2,1)}) %reduce-scatter.3.cloned.1.call-update) | async-done | bytes 2097168 | tf_op jit(solution)/shard_map/reduce_scatter | solution.py:74
  509.7 3.3 multiply_convert_fusion.1
  (10 shorter events, 0.0 us)
Async XLA Ops:
  7.2 1.7 copy-start
  7.2 90.6 %all-gather.5.cloned.1.call-start = ((), (), s32[]{:S(2)}) async-start(), calls=%async_computation.4 | async-start | bytes 4325376 | tf_op jit(solution)/shard_map/all_gather | solution.py:29
  24.3 7.2 %all-to-all-start.1 = ((bf16[4,1,1]{2,1,0:T(2,128)(2,1)}), bf16[4,1,1]{2,1,0:T(2,128)(2,1)S(1)}, u32[]{:S(2)}, u32[]{:S(2)}) async-start(bf16[4,1,1]{2,1,0:T(2,128)(2,1)} %copy.17), calls=%async_computation.1 | async-start | bytes 4096 | tf_op jit(solution)/shard_map/all_to_all | solution.py:26
  27.5 281.2 %all-gather.7.cloned.1.call-start = ((), (), s32[]{:S(2)}) async-start(), calls=%async_computation.7 | async-start | bytes 69206016 | tf_op jit(solution)/shard_map/all_gather | solution.py:49
  105.1 6.2 %copy-start.3 = (f32[2,4096]{1,0:T(2,128)S(1)}, f32[2,4096]{1,0:T(2,128)}, u32[]{:S(2)}) copy-start(f32[2,4096]{1,0:T(2,128)} %param.13) | copy-start | bytes 98308
  111.1 332.6 %reduce-scatter.5.cloned.1.call-start = ((), (), s32[]{:S(2)}) async-start(), calls=%async_computation.6 | async-start | bytes 10485760 | tf_op jit(solution)/shard_map/reduce_scatter | solution.py:77
  336.0 1.9 copy-start.2
  346.4 163.3 %reduce-scatter.3.cloned.1.call-start = ((), (), s32[]{:S(2)}) async-start(), calls=%async_computation.5 | async-start | bytes 10485760 | tf_op jit(solution)/shard_map/reduce_scatter | solution.py:74
  442.9 70.1 %copy-start.1 = (bf16[5,8192]{1,0:T(8,128)(2,1)S(1)}, bf16[5,8192]{1,0:T(8,128)(2,1)}, u32[]{:S(2)}) copy-start(bf16[5,8192]{1,0:T(8,128)(2,1)} %param.7) | copy-start | bytes 245764
Sparse Core Ops, SparseCore 0:
  21.8 47.3 all-gather.4
  111.2 197.4 all-gather.6
  346.5 80.7 reduce-scatter.4
  429.6 80.0 reduce-scatter.2
